TPU v7x, 32 devices: a whole 2x2x4 slice. The times are simulated.
32 devices in a mesh: rows: 8 (over z, x), strips: 4 (over y, core).
Axes of the slice: x: 2, y: 2, z: 4, core: 2. Of those that a mesh axis runs over, the one named last changes fastest.
Arguments:
- tokens: bfloat16 [8, 24, 64, 1280], P('rows', None, 'strips'), may hold values from -8 to 8
- stale_kv: bfloat16 [8, 2, 1536, 1280], P('rows', None, 'strips'), may hold values from -180 to 180
- stale_moments: float32 [8, 4, 2, 32], P('rows', 'strips'), as said below
- norm_gain: float32 [1280], replicated, may hold values from 0.1 to 1.9
- norm_bias: float32 [1280], replicated, may hold values from -3 to 3
- w_query: bfloat16 [1280, 1280], P('rows'), may hold values from -0.33398438 to 0.33398438
- w_key: bfloat16 [1280, 1280], P('rows'), may hold values from -0.1953125 to 0.1953125
- w_value: bfloat16 [1280, 1280], P('rows'), may hold values from -0.15625 to 0.15625
- w_out: bfloat16 [1280, 1280], P('rows'), may hold values from -0.33398438 to 0.33398438
Outputs:
- attended: bfloat16 [8, 24, 64, 1280], P('rows', None, 'strips')
- fresh_kv: bfloat16 [8, 2, 1536, 1280], P('rows', None, 'strips')
- fresh_sums: float32 [8, 4, 32], P('rows', 'strips')
- fresh_squares: float32 [8, 4, 32], P('rows', 'strips')
Inputs may be any that keep to these rules, and one draw needn't show every extreme that they name: `stale_moments`: each strip's entries are a sum of 15360 values and the sum of their squares.
All inputs are finite; a program needn't handle non-finite values.
Results may differ from a plain program's by a relative error of at most 0.0075.
The roundings to bfloat16 on the way count: a program that leaves them out, or rounds other values in their place, can miss the bound.
Values may be sent and summed in bfloat16 or wider, within the bound.
No kernel may reach another device: no remote copies, remote signals or barrier semaphores. Data moves between devices by JAX's collectives and lax.ppermute only.
A program may use at most 128 MiB of HBM per device.

v0:
```python
import jax
import jax.numpy as jnp
from jax import lax
from jax.sharding import PartitionSpec as P

HEADS = 20
HEAD = 64


def fold_keys(carry, piece, query_heads, own_start, own_count):
    top_score, total, weighted = carry
    count = piece.shape[1]
    heads = query_heads.shape[0]
    size = query_heads.shape[2]
    keys_part = piece[0].reshape(count, heads, size).transpose(1, 0, 2)
    vals_part = piece[1].reshape(count, heads, size).transpose(1, 0, 2)
    places = jnp.arange(count, dtype=jnp.int32)
    inside = (places >= own_start) & (places < own_start + own_count)

    def per_head(items):
        head_top, head_total, head_sum, head_query, head_keys, head_vals = items
        scores = jnp.dot(head_query, head_keys.T, preferred_element_type=jnp.float32)
        scores = jnp.where(inside[None, :], jnp.float32(-1e30), scores)
        new_top = jnp.maximum(head_top, scores.max(axis=-1))
        factor = jnp.exp(head_top - new_top)
        weights = jnp.exp(scores - new_top[:, None])
        upper = weights.astype(jnp.bfloat16)
        lower = (weights - upper.astype(jnp.float32)).astype(jnp.bfloat16)
        head_total = head_total * factor + weights.sum(axis=-1)
        product = jnp.dot(upper, head_vals, preferred_element_type=jnp.float32) + jnp.dot(
            lower, head_vals, preferred_element_type=jnp.float32
        )
        head_sum = head_sum * factor[:, None] + product
        return (new_top, head_total, head_sum)

    return lax.map(per_head, (top_score, total, weighted, query_heads, keys_part, vals_part))


def shards(tokens, stale_kv, stale_moments, norm_gain, norm_bias, w_query, w_key, w_value, w_out):
    band, width, chans = (tokens.shape[1], tokens.shape[2], tokens.shape[3])
    tok_count = band * width
    groups = stale_moments.shape[3]
    per_group = chans // groups
    strips = lax.axis_size("strips")
    flat = tokens.reshape(tok_count, chans).astype(jnp.float32)
    grouped = flat.reshape(tok_count, groups, per_group)
    fresh = jnp.stack([grouped.sum(axis=(0, 2)), (grouped * grouped).sum(axis=(0, 2))])
    own_moments = stale_moments[0]
    own_kv = stale_kv[0]
    totals = lax.psum(own_moments[0], "strips")
    mixed = totals - own_moments[0] + fresh
    count = float(tok_count * strips * per_group)
    mean = mixed[0] / count
    var = mixed[1] / count - mean * mean
    rstd = lax.rsqrt(var + 1e-05)
    normed = ((grouped - mean[None, :, None]) * rstd[None, :, None]).reshape(tok_count, chans)
    normed = (normed * norm_gain + norm_bias).astype(jnp.bfloat16)
    strip_index = lax.axis_index("strips")
    pieces = (
        lax.all_gather(w_query, "rows", axis=0, tiled=True),
        lax.all_gather(w_key, "rows", axis=0, tiled=True),
        lax.all_gather(w_value, "rows", axis=0, tiled=True),
    )
    columns = normed
    query_sum, key_sum, value_sum = tuple(
        (jnp.dot(columns, piece, preferred_element_type=jnp.float32) for piece in pieces)
    )
    query = (query_sum * (1.0 / HEAD**0.5)).astype(jnp.bfloat16)
    key = key_sum.astype(jnp.bfloat16)
    value = value_sum.astype(jnp.bfloat16)
    fresh_kv = jnp.stack([key, value])
    query_heads = query.reshape(tok_count, HEADS, HEAD).transpose(1, 0, 2)
    start_carry = (
        jnp.full((HEADS, tok_count), -1e30, jnp.float32),
        jnp.zeros((HEADS, tok_count), jnp.float32),
        jnp.zeros((HEADS, tok_count, HEAD), jnp.float32),
    )
    carry = fold_keys(start_carry, fresh_kv, query_heads, 0, 0)
    own_start = strip_index * tok_count
    top_score, total, weighted = fold_keys(
        carry,
        lax.all_gather(own_kv, "strips", axis=1, tiled=True),
        query_heads,
        own_start,
        tok_count,
    )
    heads_out = (
        (weighted / total[..., None])
        .transpose(1, 0, 2)
        .reshape(tok_count, HEADS * HEAD)
        .astype(jnp.bfloat16)
    )
    columns = heads_out
    attended = jnp.dot(
        columns,
        lax.all_gather(w_out, "rows", axis=0, tiled=True),
        preferred_element_type=jnp.float32,
    )
    attended = attended.astype(jnp.bfloat16)
    return (
        attended.reshape(1, band, width, chans),
        fresh_kv[None],
        fresh[0][None, None],
        fresh[1][None, None],
    )


def solution(mesh):
    in_specs = (
        P("rows", None, "strips", None),
        P("rows", None, "strips", None),
        P("rows", "strips", None, None),
        P(),
        P(),
        P("rows", None),
        P("rows", None),
        P("rows", None),
        P("rows", None),
    )
    out_specs = (
        P("rows", None, "strips", None),
        P("rows", None, "strips", None),
        P("rows", "strips", None),
        P("rows", "strips", None),
    )
    return jax.shard_map(shards, mesh=mesh, in_specs=in_specs, out_specs=out_specs, check_vma=False)
```

profile of v0, /device:TPU:0, one launch (start us, length us, event | category | flops | bytes accessed | tf_op | source)
XLA Modules:
  0.0 416.8 jit_solution(2687440719954865516)
XLA Ops:
  9.4 4.0 copy.32
  15.1 8.4 %psum.7 = f32[2,32]{1,0:T(2,128)S(1)} all-reduce(f32[2,32]{1,0:T(2,128)S(1)} %bitcast.135), channel_id=1, replica_groups=mesh['rows'=8,'strips'=4] {'strips'}, use_global_device_ids=true, to_apply=%region_0.0 | all-reduce | flops 64 | bytes 512 | tf_op jit(solution)/shard_map/psum | solution.py:50
  24.5 49.8 %all-gather.7.cloned.1.call-done = bf16[1280,1280]{1,0:T(8,128)(2,1)} async-done(((bf16[160,1280]{1,0:T(8,128)(2,1)}), bf16[1280,1280]{1,0:T(8,128)(2,1)}) %all-gather.7.cloned.1.call-update) | async-done | bytes 3276816 | tf_op jit(solution)/shard_map/all_gather | solution.py:60
  74.4 3.4 fusion.49
  79.5 57.2 %all-gather.9.cloned.1.call-done = bf16[1280,1280]{1,0:T(8,128)(2,1)} async-done(((bf16[160,1280]{1,0:T(8,128)(2,1)}), bf16[1280,1280]{1,0:T(8,128)(2,1)}) %all-gather.9.cloned.1.call-update) | async-done | bytes 3276816 | tf_op jit(solution)/shard_map/all_gather | solution.py:61
  136.7 3.7 convolution_convert_fusion.2
  141.7 57.4 %all-gather.11.cloned.1.call-done = bf16[1280,1280]{1,0:T(8,128)(2,1)} async-done(((bf16[160,1280]{1,0:T(8,128)(2,1)}), bf16[1280,1280]{1,0:T(8,128)(2,1)}) %all-gather.11.cloned.1.call-update) | async-done | bytes 3276816 | tf_op jit(solution)/shard_map/all_gather | solution.py:62
  199.1 4.7 %convolution_convert_fusion.1 = bf16[384,1280]{1,0:T(8,128)(2,1)} fusion(bf16[384,1280]{1,0:T(8,128)(2,1)} %copy-done.2, bf16[1280,1280]{1,0:T(8,128)(2,1)} %all-gather.11.cloned.1.call-done), kind=kOutput, calls=%fused_computation.65 | convolution fusion | flops 1258782720 | bytes 5242880 | tf_op jit(solution)/shard_map/dot_general | solution.py:66
  203.7 2.2 copy.28
  206.0 1.5 broadcast.114.clone
  207.5 82.3 %while.28 = (s32[]{:T(128)}, f32[20,384]{1,0:T(8,128)S(1)}, f32[20,384]{1,0:T(8,128)S(1)}, f32[20,384,64]{1,2,0:T(8,128)}, bf16[20,384,64]{2,1,0:T(8,128)(2,1)S(...) while((s32[]{:T(128)}, f32[20,384]{1,0:T(8,128)S(1)}, ...), condition=%wide.region_8.9_spmd, body=%wide.region_5.8_spmd.sunk | while | flops 58148352 | bytes 2930277 | solution.py:36
  209.7 1.7 fusion.90
  213.8 1.7 fusion.90
  217.9 1.7 fusion.90
  222.0 1.7 fusion.90
  226.1 1.7 fusion.90
  230.2 1.7 fusion.90
  234.4 1.7 fusion.90
  238.5 1.7 fusion.90
  242.6 1.7 fusion.90
  246.7 1.7 fusion.90
  250.8 1.7 fusion.90
  254.9 1.7 fusion.90
  259.0 1.7 fusion.90
  263.2 1.7 fusion.90
  267.3 1.7 fusion.90
  271.4 1.7 fusion.90
  275.5 1.7 fusion.90
  279.6 1.7 fusion.90
  283.8 1.7 fusion.90
  287.9 1.7 fusion.90
  289.9 3.4 maximum_bitcast_fusion
  293.2 5.6 %fusion.58 = (bf16[1,1,1536,1280]{2,3,1,0:T(8,128)(2,1)}, bf16[1,1,1536,1280]{2,3,1,0:T(8,128)(2,1)}) fusion(bf16[1,2,1536,1280]{2,3,1,0:T(8,128)(2,1)} %all-gather.15.cloned.1.call-done), kind=kLoop, calls=%fused_computation.83 | loop fusion | bytes 15728640 | tf_op jit(solution)/shard_map/slice | solution.py:16
  299.0 106.6 %while.29 = (s32[]{:T(128)}, f32[20,384]{1,0:T(8,128)S(1)}, f32[20,384,64]{1,2,0:T(8,128)S(1)}, f32[20,384]{1,0:T(8,128)S(1)}, f32[20,384]{1,0:T(8,128)S(1)}, /*...) while((s32[]{:T(128)}, f32[20,384]{1,0:T(8,128)S(1)}, ...), condition=%wide.region_12.13_spmd.clone, body=%wide.region_9.12_spmd.clone.sunk | while | flops 233060352 | bytes 10554513 | solution.py:36
  300.6 1.5 fusion.99
  302.2 1.6 fusion.100
  307.5 1.6 fusion.100
  311.3 1.5 fusion.99
  312.8 1.6 fusion.100
  318.2 1.6 fusion.100
  321.9 1.5 fusion.99
  323.5 1.6 fusion.100
  327.3 1.5 fusion.99
  328.8 1.6 fusion.100
  332.6 1.5 fusion.99
  334.2 1.6 fusion.100
  337.9 1.5 fusion.99
  339.5 1.6 fusion.100
  343.3 1.5 fusion.99
  344.8 1.6 fusion.100
  348.6 1.5 fusion.99
  350.2 1.6 fusion.100
  353.9 1.5 fusion.99
  355.5 1.6 fusion.100
  360.8 1.6 fusion.100
  366.1 1.6 fusion.100
  371.5 1.6 fusion.100
  376.8 1.6 fusion.100
  382.1 1.6 fusion.100
  387.5 1.6 fusion.100
  392.8 1.6 fusion.100
  398.1 1.6 fusion.100
  403.5 1.6 fusion.100
  405.9 4.4 %convolution_convert_fusion = bf16[384,1280]{1,0:T(8,128)(2,1)} fusion(bf16[384,1280]{0,1:T(8,128)(2,1)S(1)} %bitcast.134, bf16[1280,1280]{1,0:T(8,128)(2,1)} %all-gather.13.cloned.1.call-done), kind=kOutput, calls=%fused_computation.64 | convolution fusion | flops 1258782720 | bytes 5242880 | tf_op jit(solution)/shard_map/dot_general | solution.py:94
  (360 shorter events, 114.8 us)
Async XLA Ops:
  7.2 67.2 %all-gather.7.cloned.1.call-start = ((), (), s32[]{:S(2)}) async-start(), calls=%async_computation | async-start | bytes 3686400 | tf_op jit(solution)/shard_map/all_gather | solution.py:60
  7.9 128.8 %all-gather.9.cloned.1.call-start = ((), (), s32[]{:S(2)}) async-start(), calls=%async_computation.1 | async-start | bytes 3686400 | tf_op jit(solution)/shard_map/all_gather | solution.py:61
  8.6 190.4 %all-gather.11.cloned.1.call-start = ((), (), s32[]{:S(2)}) async-start(), calls=%async_computation.2 | async-start | bytes 3686400 | tf_op jit(solution)/shard_map/all_gather | solution.py:62
  9.4 283.9 %all-gather.15.cloned.1.call-start = ((), (), s32[]{:S(2)}) async-start(), calls=%async_computation.4 | async-start | bytes 9830400 | tf_op jit(solution)/shard_map/all_gather | solution.py:82
  13.4 1.2 copy-start.1
  13.4 1.7 copy-start.5
  13.4 10.7 %copy-start.3 = (f32[1280]{0:T(1024)S(1)}, f32[1280]{0:T(1024)}, u32[]{:S(2)}) copy-start(f32[1280]{0:T(1024)} %param.17) | copy-start | bytes 15364
  13.4 10.7 %copy-start.4 = (f32[1280]{0:T(1024)S(1)}, f32[1280]{0:T(1024)}, u32[]{:S(2)}) copy-start(f32[1280]{0:T(1024)} %param.16) | copy-start | bytes 15364
  13.5 392.4 %all-gather.13.cloned.1.call-start = ((), (), s32[]{:S(2)}) async-start(), calls=%async_computation.3 | async-start | bytes 3686400 | tf_op jit(solution)/shard_map/all_gather | solution.py:96
  23.6 54.1 %copy-start.6 = (f32[32]{0:T(128)}, f32[32]{0:T(128)S(1)}, u32[]{:S(2)}) copy-start(f32[32]{0:T(128)S(1)} %reduce_sum.58) | copy-start | bytes 388
  23.7 54.0 %copy-start.7 = (f32[32]{0:T(128)}, f32[32]{0:T(128)S(1)}, u32[]{:S(2)}) copy-start(f32[32]{0:T(128)S(1)} %reduce_sum.61) | copy-start | bytes 388
  24.5 53.2 %copy-start.2 = (bf16[384,1280]{1,0:T(8,128)(2,1)}, bf16[384,1280]{1,0:T(8,128)(2,1)S(1)}, u32[]{:S(2)}) copy-start(bf16[384,1280]{1,0:T(8,128)(2,1)S(1)} %fusion.53) | copy-start | bytes 2949124
  289.9 3.4 copy-start
Sparse Core Ops, SparseCore 0:
  10.2 64.1 all-gather.6
  76.5 60.1 all-gather.8
  138.9 60.1 all-gather.10
  200.5 53.8 all-gather.14
  256.4 61.4 all-gather.12
where the time goes:
time: 422 us; the launch traced here: 417 us
  matrix products  186 us (44%)
  waiting for transfers between devices  167 us (40%)
  local copies, waits for them, and re-layouts  21.4 us (5%)
  other arithmetic  17.5 us (4%)
  between operations  14 us (3%)
  blocking collectives  8.4 us (2%)
    dot_general x40, matrix products, per_head(): jnp.dot(lower, head_vals, preferred_element_type=jnp.float32)  66.4 us
    all_gather x1, waiting for transfers between devices, shards(): lax.all_gather(w_value, 'rows', axis=0, tiled=True)  57.4 us
    all_gather x1, waiting for transfers between devices, shards(): lax.all_gather(w_key, 'rows', axis=0, tiled=True)  57.2 us
    dot_general x40, matrix products, per_head(): jnp.dot(head_query, head_keys.T, preferred_element_type=jnp.float32)  52.4 us
    dot_general x40, matrix products, per_head(): jnp.dot(upper, head_vals, preferred_element_type=jnp.float32)  51.4 us
    all_gather x1, waiting for transfers between devices, shards(): lax.all_gather(w_query, 'rows', axis=0, tiled=True)  49.8 us
    reduce_sum x40, other arithmetic, per_head(): head_total = head_total * factor + weights.sum(axis=-1)  11.8 us
    dot_general x3, matrix products, shards(): jnp.dot(columns, piece, preferred_element_type=jnp.float32)  11.7 us
  transfers between devices with their start and end apart: 5, of which 3 were waited for; matrix products, arithmetic and copies ran while one was open for 53% of the time, Pallas kernels for 0%

commit v1 on v0

--- a/solution.py
+++ b/solution.py
@@ -5,6 +5,17 @@
 
 HEADS = 20
 HEAD = 64
+
+
+def collect(shard, axis, dim):
+    ways = lax.axis_size(axis)
+    pieces = [shard]
+    for far in range(1, ways):
+        pieces.append(
+            lax.ppermute(pieces[far - 1], axis, [(d, (d - 1) % ways) for d in range(ways)])
+        )
+    line = jnp.concatenate(pieces, axis=dim)
+    return jnp.roll(line, lax.axis_index(axis) * shard.shape[dim], axis=dim)
 
 
 def fold_keys(carry, piece, query_heads, own_start, own_count):
@@ -58,7 +69,7 @@
     strip_index = lax.axis_index("strips")
     pieces = (
         lax.all_gather(w_query, "rows", axis=0, tiled=True),
-        lax.all_gather(w_key, "rows", axis=0, tiled=True),
+        collect(w_key, "rows", 0),
         lax.all_gather(w_value, "rows", axis=0, tiled=True),
     )
     columns = normed

time: 422 us -> 400 us (0.948)
  waiting for transfers between devices: 167 us -> 114 us
  starting transfers between devices: 0.19 us -> 37.3 us
    ppermute x0 -> x7, waiting for transfers between devices: none -> 81.5 us  [collect(): lax.ppermute(pieces[far - 1], axis, [(d, (d - 1) % ways) for d in range(w...]
    all_gather x1 -> x0, waiting for transfers between devices: 57.2 us -> none  [shards(): lax.all_gather(w_key, 'rows', axis=0, tiled=True)]
    all_gather x1, waiting for transfers between devices: 49.8 us -> 0.01 us  [shards(): lax.all_gather(w_query, 'rows', axis=0, tiled=True)]
    ppermute x0 -> x7, starting transfers between devices: none -> 37.1 us  [collect(): lax.ppermute(pieces[far - 1], axis, [(d, (d - 1) % ways) for d in range(w...]
    all_gather x1, waiting for transfers between devices: 57.4 us -> 31 us  [shards(): lax.all_gather(w_value, 'rows', axis=0, tiled=True)]
  transfers between devices with their start and end apart: 5 -> 11, of which waited for: 3 -> 8; matrix products, arithmetic and copies ran while one was open for 53% -> 55% of each run, Pallas kernels for 0% -> 0%
where the time goes in v1:
time: 400 us; the launch traced here: 396 us
  matrix products  183 us (46%)
  waiting for transfers between devices  114 us (28%)
  starting transfers between devices  37.3 us (9%)
  local copies, waits for them, and re-layouts  20.5 us (5%)
  other arithmetic  17.5 us (4%)
  between operations  14.2 us (4%)
  blocking collectives  6.63 us (2%)
    ppermute x7, waiting for transfers between devices, collect(): lax.ppermute(pieces[far - 1], axis, [(d, (d - 1) % ways) for d in range(w...  81.5 us
    dot_general x40, matrix products, per_head(): jnp.dot(lower, head_vals, preferred_element_type=jnp.float32)  66.4 us
    dot_general x40, matrix products, per_head(): jnp.dot(head_query, head_keys.T, preferred_element_type=jnp.float32)  52.4 us
    dot_general x40, matrix products, per_head(): jnp.dot(upper, head_vals, preferred_element_type=jnp.float32)  51.4 us
    ppermute x7, starting transfers between devices, collect(): lax.ppermute(pieces[far - 1], axis, [(d, (d - 1) % ways) for d in range(w...  37.1 us
    all_gather x1, waiting for transfers between devices, shards(): lax.all_gather(w_value, 'rows', axis=0, tiled=True)  31 us
    reduce_sum x40, other arithmetic, per_head(): head_total = head_total * factor + weights.sum(axis=-1)  11.8 us
    dot_general x3, matrix products, shards(): jnp.dot(columns, piece, preferred_element_type=jnp.float32)  8.82 us
  transfers between devices with their start and end apart: 11, of which 8 were waited for; matrix products, arithmetic and copies ran while one was open for 55% of the time, Pallas kernels for 0%

profile of v1, /device:TPU:0, one launch (start us, length us, event | category | flops | bytes accessed | tf_op | source)
XLA Modules:
  0.0 395.5 jit_solution(3391208759953531299)
XLA Ops:
  8.7 4.1 %copy.32 = bf16[1,2,384,1280]{2,3,1,0:T(8,128)(2,1)} copy(bf16[1,2,384,1280]{3,2,1,0:T(8,128)(2,1)} %param.14) | data formatting | bytes 3932160 | tf_op args[1]
  12.9 6.1 %collective-permute-start = (bf16[160,1280]{1,0:T(8,128)(2,1)S(1)}, bf16[160,1280]{1,0:T(8,128)(2,1)S(1)}, u32[]{:S(2)}, u32[]{:S(2)}) collective-permute-start(bf16[160,1280]{1,0:T(8,128)(2,1)S(1)} %copy-done.5), channel_id=1, source_target_pairs={{0,28},{4,0},{8,4},{12,8},{16,12},{20,16},{24,20},{28,24},{1,29},{... | collective-permute-start | bytes 1228808 | tf_op jit(solution)/shard_map/ppermute | solution.py:15
  19.8 6.6 %psum.7 = f32[2,32]{1,0:T(2,128)S(1)} all-reduce(f32[2,32]{1,0:T(2,128)S(1)} %bitcast.134), channel_id=1, replica_groups=mesh['rows'=8,'strips'=4] {'strips'}, use_global_device_ids=true, to_apply=%region_0.0 | all-reduce | flops 64 | bytes 512 | tf_op jit(solution)/shard_map/psum | solution.py:61
  26.4 8.4 %collective-permute-done = bf16[160,1280]{1,0:T(8,128)(2,1)S(1)} collective-permute-done((bf16[160,1280]{1,0:T(8,128)(2,1)S(1)}, bf16[160,1280]{1,0:T(8,128)(2,1)S(1)}, u32[]{:S(2)}, u32[]{:S(2)}) %collective-permute-start) | collective-permute-done | bytes 409632 | tf_op jit(solution)/shard_map/ppermute | solution.py:15
  34.8 5.2 %collective-permute-start.1 = (bf16[160,1280]{1,0:T(8,128)(2,1)S(1)}, bf16[160,1280]{1,0:T(8,128)(2,1)S(1)}, u32[]{:S(2)}, u32[]{:S(2)}) collective-permute-start(bf16[160,1280]{1,0:T(8,128)(2,1)S(1)} %collective-permute-done), channel_id=1, source_target_pairs={{0,28},{4,0},{8,4},{12,8},{16,12},{20,16},{24,20},{28,24},{1,29},{... | collective-permute-start | bytes 1228808 | tf_op jit(solution)/shard_map/ppermute | solution.py:15
  40.2 9.4 %collective-permute-done.1 = bf16[160,1280]{1,0:T(8,128)(2,1)S(1)} collective-permute-done((bf16[160,1280]{1,0:T(8,128)(2,1)S(1)}, bf16[160,1280]{1,0:T(8,128)(2,1)S(1)}, u32[]{:S(2)}, u32[]{:S(2)}) %collective-permute-start.1) | collective-permute-done | bytes 409632 | tf_op jit(solution)/shard_map/ppermute | solution.py:15
  49.7 5.2 %collective-permute-start.2 = (bf16[160,1280]{1,0:T(8,128)(2,1)S(1)}, bf16[160,1280]{1,0:T(8,128)(2,1)S(1)}, u32[]{:S(2)}, u32[]{:S(2)}) collective-permute-start(bf16[160,1280]{1,0:T(8,128)(2,1)S(1)} %collective-permute-done.1), channel_id=1, source_target_pairs={{0,28},{4,0},{8,4},{12,8},{16,12},{20,16},{24,20},{28,24},{1,29},{... | collective-permute-start | bytes 1228808 | tf_op jit(solution)/shard_map/ppermute | solution.py:15
  55.1 16.3 %collective-permute-done.2 = bf16[160,1280]{1,0:T(8,128)(2,1)S(1)} collective-permute-done((bf16[160,1280]{1,0:T(8,128)(2,1)S(1)}, bf16[160,1280]{1,0:T(8,128)(2,1)S(1)}, u32[]{:S(2)}, u32[]{:S(2)}) %collective-permute-start.2) | collective-permute-done | bytes 409632 | tf_op jit(solution)/shard_map/ppermute | solution.py:15
  71.3 5.2 %collective-permute-start.3 = (bf16[160,1280]{1,0:T(8,128)(2,1)S(1)}, bf16[160,1280]{1,0:T(8,128)(2,1)S(1)}, u32[]{:S(2)}, u32[]{:S(2)}) collective-permute-start(bf16[160,1280]{1,0:T(8,128)(2,1)S(1)} %collective-permute-done.2), channel_id=1, source_target_pairs={{0,28},{4,0},{8,4},{12,8},{16,12},{20,16},{24,20},{28,24},{1,29},{... | collective-permute-start | bytes 1228808 | tf_op jit(solution)/shard_map/ppermute | solution.py:15
  76.9 16.5 %collective-permute-done.3 = bf16[160,1280]{1,0:T(8,128)(2,1)S(1)} collective-permute-done((bf16[160,1280]{1,0:T(8,128)(2,1)S(1)}, bf16[160,1280]{1,0:T(8,128)(2,1)S(1)}, u32[]{:S(2)}, u32[]{:S(2)}) %collective-permute-start.3) | collective-permute-done | bytes 409632 | tf_op jit(solution)/shard_map/ppermute | solution.py:15
  93.4 5.2 %collective-permute-start.4 = (bf16[160,1280]{1,0:T(8,128)(2,1)S(1)}, bf16[160,1280]{1,0:T(8,128)(2,1)S(1)}, u32[]{:S(2)}, u32[]{:S(2)}) collective-permute-start(bf16[160,1280]{1,0:T(8,128)(2,1)S(1)} %collective-permute-done.3), channel_id=1, source_target_pairs={{0,28},{4,0},{8,4},{12,8},{16,12},{20,16},{24,20},{28,24},{1,29},{... | collective-permute-start | bytes 1228808 | tf_op jit(solution)/shard_map/ppermute | solution.py:15
  98.6 7.8 %collective-permute-done.4 = bf16[160,1280]{1,0:T(8,128)(2,1)S(1)} collective-permute-done((bf16[160,1280]{1,0:T(8,128)(2,1)S(1)}, bf16[160,1280]{1,0:T(8,128)(2,1)S(1)}, u32[]{:S(2)}, u32[]{:S(2)}) %collective-permute-start.4) | collective-permute-done | bytes 409632 | tf_op jit(solution)/shard_map/ppermute | solution.py:15
  106.4 5.2 %collective-permute-start.5 = (bf16[160,1280]{1,0:T(8,128)(2,1)S(1)}, bf16[160,1280]{1,0:T(8,128)(2,1)S(1)}, u32[]{:S(2)}, u32[]{:S(2)}) collective-permute-start(bf16[160,1280]{1,0:T(8,128)(2,1)S(1)} %collective-permute-done.4), channel_id=1, source_target_pairs={{0,28},{4,0},{8,4},{12,8},{16,12},{20,16},{24,20},{28,24},{1,29},{... | collective-permute-start | bytes 1228808 | tf_op jit(solution)/shard_map/ppermute | solution.py:15
  111.6 6.1 %collective-permute-done.5 = bf16[160,1280]{1,0:T(8,128)(2,1)S(1)} collective-permute-done((bf16[160,1280]{1,0:T(8,128)(2,1)S(1)}, bf16[160,1280]{1,0:T(8,128)(2,1)S(1)}, u32[]{:S(2)}, u32[]{:S(2)}) %collective-permute-start.5) | collective-permute-done | bytes 409632 | tf_op jit(solution)/shard_map/ppermute | solution.py:15
  117.8 5.2 %collective-permute-start.6 = (bf16[160,1280]{1,0:T(8,128)(2,1)S(1)}, bf16[160,1280]{1,0:T(8,128)(2,1)S(1)}, u32[]{:S(2)}, u32[]{:S(2)}) collective-permute-start(bf16[160,1280]{1,0:T(8,128)(2,1)S(1)} %collective-permute-done.5), channel_id=1, source_target_pairs={{0,28},{4,0},{8,4},{12,8},{16,12},{20,16},{24,20},{28,24},{1,29},{... | collective-permute-start | bytes 1228808 | tf_op jit(solution)/shard_map/ppermute | solution.py:15
  123.0 17.0 %collective-permute-done.6 = bf16[160,1280]{1,0:T(8,128)(2,1)S(1)} collective-permute-done((bf16[160,1280]{1,0:T(8,128)(2,1)S(1)}, bf16[160,1280]{1,0:T(8,128)(2,1)S(1)}, u32[]{:S(2)}, u32[]{:S(2)}) %collective-permute-start.6) | collective-permute-done | bytes 409632 | tf_op jit(solution)/shard_map/ppermute | solution.py:15
  143.1 3.7 fusion.51
  148.6 31.0 %all-gather.8.cloned.1.call-done = bf16[1280,1280]{1,0:T(8,128)(2,1)} async-done(((bf16[160,1280]{1,0:T(8,128)(2,1)}), bf16[1280,1280]{1,0:T(8,128)(2,1)}) %all-gather.8.cloned.1.call-update) | async-done | bytes 3276816 | tf_op jit(solution)/shard_map/all_gather | solution.py:73
  179.5 3.7 convolution_convert_fusion.1
  186.1 82.5 %while.28 = (s32[]{:T(128)}, f32[20,384]{1,0:T(8,128)S(1)}, f32[20,384]{1,0:T(8,128)S(1)}, f32[20,384,64]{1,2,0:T(8,128)}, bf16[20,384,64]{2,1,0:T(8,128)(2,1)S(...) while((s32[]{:T(128)}, f32[20,384]{1,0:T(8,128)S(1)}, ...), condition=%wide.region_8.9_spmd, body=%wide.region_5.8_spmd.sunk | while | flops 58148352 | bytes 2930277 | solution.py:47
  188.4 1.7 fusion.95
  192.5 1.7 fusion.95
  196.6 1.7 fusion.95
  200.8 1.7 fusion.95
  204.9 1.7 fusion.95
  209.0 1.7 fusion.95
  213.1 1.7 fusion.95
  217.2 1.7 fusion.95
  221.3 1.7 fusion.95
  225.5 1.7 fusion.95
  229.6 1.7 fusion.95
  233.7 1.7 fusion.95
  237.8 1.7 fusion.95
  241.9 1.7 fusion.95
  246.0 1.7 fusion.95
  250.2 1.7 fusion.95
  254.3 1.7 fusion.95
  258.4 1.7 fusion.95
  262.5 1.7 fusion.95
  266.6 1.7 fusion.95
  268.6 3.4 maximum_bitcast_fusion
  272.0 5.6 %fusion.64 = (bf16[1,1,1536,1280]{2,3,1,0:T(8,128)(2,1)}, bf16[1,1,1536,1280]{2,3,1,0:T(8,128)(2,1)}) fusion(bf16[1,2,1536,1280]{2,3,1,0:T(8,128)(2,1)} %all-gather.12.cloned.1.call-done), kind=kLoop, calls=%fused_computation.102 | loop fusion | bytes 15728640 | tf_op jit(solution)/shard_map/slice | solution.py:27
  277.8 106.6 %while.29 = (s32[]{:T(128)}, f32[20,384]{1,0:T(8,128)S(1)}, f32[20,384,64]{1,2,0:T(8,128)S(1)}, f32[20,384]{1,0:T(8,128)S(1)}, f32[20,384]{1,0:T(8,128)S(1)}, /*...) while((s32[]{:T(128)}, f32[20,384]{1,0:T(8,128)S(1)}, ...), condition=%wide.region_12.13_spmd.clone, body=%wide.region_9.12_spmd.clone.sunk | while | flops 233060352 | bytes 10554513 | solution.py:47
  280.9 1.6 fusion.105
  286.2 1.6 fusion.105
  291.6 1.6 fusion.105
  296.9 1.6 fusion.105
  302.2 1.6 fusion.105
  307.5 1.6 fusion.105
  312.9 1.6 fusion.105
  318.2 1.6 fusion.105
  323.5 1.6 fusion.105
  328.9 1.6 fusion.105
  334.2 1.6 fusion.105
  339.5 1.6 fusion.105
  344.9 1.6 fusion.105
  350.2 1.6 fusion.105
  355.5 1.6 fusion.105
  360.9 1.6 fusion.105
  366.2 1.6 fusion.105
  371.5 1.6 fusion.105
  376.8 1.6 fusion.105
  382.2 1.6 fusion.105
  384.6 4.4 %convolution_convert_fusion = bf16[384,1280]{1,0:T(8,128)(2,1)} fusion(bf16[384,1280]{0,1:T(8,128)(2,1)S(1)} %bitcast.133, bf16[1280,1280]{1,0:T(8,128)(2,1)} %all-gather.10.cloned.1.call-done), kind=kOutput, calls=%fused_computation.67 | convolution fusion | flops 1258782720 | bytes 5242880 | tf_op jit(solution)/shard_map/dot_general | solution.py:105
  (395 shorter events, 131.8 us)
Async XLA Ops:
  7.2 5.8 %copy-start.5 = (bf16[160,1280]{1,0:T(8,128)(2,1)S(1)}, bf16[160,1280]{1,0:T(8,128)(2,1)}, u32[]{:S(2)}) copy-start(bf16[160,1280]{1,0:T(8,128)(2,1)} %param.19) | copy-start | bytes 1228804
  7.2 136.0 %all-gather.6.cloned.1.call-start = ((), (), s32[]{:S(2)}) async-start(), calls=%async_computation | async-start | bytes 3686400 | tf_op jit(solution)/shard_map/all_gather | solution.py:71
  7.9 11.1 %copy-start.1 = (bf16[1,24,16,1280]{3,2,1,0:T(8,128)(2,1)S(1)}, bf16[1,24,16,1280]{3,2,1,0:T(8,128)(2,1)}, u32[]{:S(2)}) copy-start(bf16[1,24,16,1280]{3,2,1,0:T(8,128)(2,1)} %param.13) | copy-start | bytes 2949124
  7.9 171.6 %all-gather.8.cloned.1.call-start = ((), (), s32[]{:S(2)}) async-start(), calls=%async_computation.1 | async-start | bytes 3686400 | tf_op jit(solution)/shard_map/all_gather | solution.py:73
  8.7 11.1 %copy-start.9 = (f32[1,1,2,32]{3,2,1,0:T(2,128)S(1)}, f32[1,1,2,32]{3,2,1,0:T(2,128)}, u32[]{:S(2)}) copy-start(f32[1,1,2,32]{3,2,1,0:T(2,128)} %param.15) | copy-start | bytes 772
  8.7 67.8 %copy-start.7 = (f32[1280]{0:T(1024)S(1)}, f32[1280]{0:T(1024)}, u32[]{:S(2)}) copy-start(f32[1280]{0:T(1024)} %param.17) | copy-start | bytes 15364
  8.7 67.8 %copy-start.8 = (f32[1280]{0:T(1024)S(1)}, f32[1280]{0:T(1024)}, u32[]{:S(2)}) copy-start(f32[1280]{0:T(1024)} %param.16) | copy-start | bytes 15364
  8.7 263.3 %all-gather.12.cloned.1.call-start = ((), (), s32[]{:S(2)}) async-start(), calls=%async_computation.3 | async-start | bytes 9830400 | tf_op jit(solution)/shard_map/all_gather | solution.py:93
  12.9 371.8 %all-gather.10.cloned.1.call-start = ((), (), s32[]{:S(2)}) async-start(), calls=%async_computation.2 | async-start | bytes 3686400 | tf_op jit(solution)/shard_map/all_gather | solution.py:107
  12.9 21.9 %collective-permute-start = (bf16[160,1280]{1,0:T(8,128)(2,1)S(1)}, bf16[160,1280]{1,0:T(8,128)(2,1)S(1)}, u32[]{:S(2)}, u32[]{:S(2)}) collective-permute-start(bf16[160,1280]{1,0:T(8,128)(2,1)S(1)} %copy-done.5), channel_id=1, source_target_pairs={{0,28},{4,0},{8,4},{12,8},{16,12},{20,16},{24,20},{28,24},{1,29},{... | collective-permute-start | bytes 1228808 | tf_op jit(solution)/shard_map/ppermute | solution.py:15
  19.6 103.3 %copy-start.10 = (f32[32]{0:T(128)}, f32[32]{0:T(128)S(1)}, u32[]{:S(2)}) copy-start(f32[32]{0:T(128)S(1)} %reduce_sum.58) | copy-start | bytes 388
  19.7 103.2 %copy-start.11 = (f32[32]{0:T(128)}, f32[32]{0:T(128)S(1)}, u32[]{:S(2)}) copy-start(f32[32]{0:T(128)S(1)} %reduce_sum.61) | copy-start | bytes 388
  34.8 14.8 %collective-permute-start.1 = (bf16[160,1280]{1,0:T(8,128)(2,1)S(1)}, bf16[160,1280]{1,0:T(8,128)(2,1)S(1)}, u32[]{:S(2)}, u32[]{:S(2)}) collective-permute-start(bf16[160,1280]{1,0:T(8,128)(2,1)S(1)} %collective-permute-done), channel_id=1, source_target_pairs={{0,28},{4,0},{8,4},{12,8},{16,12},{20,16},{24,20},{28,24},{1,29},{... | collective-permute-start | bytes 1228808 | tf_op jit(solution)/shard_map/ppermute | solution.py:15
  49.7 21.7 %collective-permute-start.2 = (bf16[160,1280]{1,0:T(8,128)(2,1)S(1)}, bf16[160,1280]{1,0:T(8,128)(2,1)S(1)}, u32[]{:S(2)}, u32[]{:S(2)}) collective-permute-start(bf16[160,1280]{1,0:T(8,128)(2,1)S(1)} %collective-permute-done.1), channel_id=1, source_target_pairs={{0,28},{4,0},{8,4},{12,8},{16,12},{20,16},{24,20},{28,24},{1,29},{... | collective-permute-start | bytes 1228808 | tf_op jit(solution)/shard_map/ppermute | solution.py:15
  71.3 22.0 %collective-permute-start.3 = (bf16[160,1280]{1,0:T(8,128)(2,1)S(1)}, bf16[160,1280]{1,0:T(8,128)(2,1)S(1)}, u32[]{:S(2)}, u32[]{:S(2)}) collective-permute-start(bf16[160,1280]{1,0:T(8,128)(2,1)S(1)} %collective-permute-done.2), channel_id=1, source_target_pairs={{0,28},{4,0},{8,4},{12,8},{16,12},{20,16},{24,20},{28,24},{1,29},{... | collective-permute-start | bytes 1228808 | tf_op jit(solution)/shard_map/ppermute | solution.py:15
  76.9 63.4 %copy-start.6 = (bf16[384,1280]{1,0:T(8,128)(2,1)}, bf16[384,1280]{1,0:T(8,128)(2,1)S(1)}, u32[]{:S(2)}) copy-start(bf16[384,1280]{1,0:T(8,128)(2,1)S(1)} %fusion.58) | copy-start | bytes 2949124
  93.4 13.0 %collective-permute-start.4 = (bf16[160,1280]{1,0:T(8,128)(2,1)S(1)}, bf16[160,1280]{1,0:T(8,128)(2,1)S(1)}, u32[]{:S(2)}, u32[]{:S(2)}) collective-permute-start(bf16[160,1280]{1,0:T(8,128)(2,1)S(1)} %collective-permute-done.3), channel_id=1, source_target_pairs={{0,28},{4,0},{8,4},{12,8},{16,12},{20,16},{24,20},{28,24},{1,29},{... | collective-permute-start | bytes 1228808 | tf_op jit(solution)/shard_map/ppermute | solution.py:15
  106.4 11.4 %collective-permute-start.5 = (bf16[160,1280]{1,0:T(8,128)(2,1)S(1)}, bf16[160,1280]{1,0:T(8,128)(2,1)S(1)}, u32[]{:S(2)}, u32[]{:S(2)}) collective-permute-start(bf16[160,1280]{1,0:T(8,128)(2,1)S(1)} %collective-permute-done.4), channel_id=1, source_target_pairs={{0,28},{4,0},{8,4},{12,8},{16,12},{20,16},{24,20},{28,24},{1,29},{... | collective-permute-start | bytes 1228808 | tf_op jit(solution)/shard_map/ppermute | solution.py:15
  117.8 22.2 %collective-permute-start.6 = (bf16[160,1280]{1,0:T(8,128)(2,1)S(1)}, bf16[160,1280]{1,0:T(8,128)(2,1)S(1)}, u32[]{:S(2)}, u32[]{:S(2)}) collective-permute-start(bf16[160,1280]{1,0:T(8,128)(2,1)S(1)} %collective-permute-done.5), channel_id=1, source_target_pairs={{0,28},{4,0},{8,4},{12,8},{16,12},{20,16},{24,20},{28,24},{1,29},{... | collective-permute-start | bytes 1228808 | tf_op jit(solution)/shard_map/ppermute | solution.py:15
  141.8 5.0 %copy-start.2 = (bf16[384,1280]{1,0:T(8,128)(2,1)}, bf16[384,1280]{1,0:T(8,128)(2,1)S(1)}, u32[]{:S(2)}) copy-start(bf16[384,1280]{1,0:T(8,128)(2,1)S(1)} %fusion.52) | copy-start | bytes 2949124
  183.2 2.9 copy-start.4
  186.1 82.5 %copy-start.3 = (bf16[384,1280]{1,0:T(8,128)(2,1)S(1)}, bf16[384,1280]{1,0:T(8,128)(2,1)}, u32[]{:S(2)}) copy-start(bf16[384,1280]{1,0:T(8,128)(2,1)} %copy-done.2) | copy-start | bytes 2949124
  268.6 8.9 %copy-start = (bf16[20,384,64]{2,1,0:T(8,128)(2,1)}, bf16[20,384,64]{2,1,0:T(8,128)(2,1)S(1)}, u32[]{:S(2)}) copy-start(bf16[20,384,64]{2,1,0:T(8,128)(2,1)S(1)} %get-tuple-element.436) | copy-start | bytes 2949124
Sparse Core Ops, SparseCore 0:
  10.2 93.3 all-gather.5
  105.7 73.7 all-gather.7
  181.1 53.9 all-gather.11
  237.2 61.2 all-gather.9
